TPU v7x, 256 devices: a whole 4x4x8 slice. The times are simulated.
256 devices in a mesh: slab: 4 (over x), panel: 64 (over z, y, core).
Axes of the slice: x: 4, y: 4, z: 8, core: 2. Of those that a mesh axis runs over, the one named last changes fastest.
Arguments:
- trial: bfloat16 [1600, 6400], P('slab', 'panel'), may hold values from -6 to 6
- integrals: bfloat16 [6400, 256, 300], P(None, 'panel'), may hold values from -0.078125 to 0.078125
- basis: bfloat16 [2, 1600, 256, 300], P(None, 'slab', 'panel'), may hold values from -0.00048828125 to 0.00048828125
- images: bfloat16 [2, 1600, 256, 300], P(None, 'slab', 'panel'), may hold values from -6 to 6
- current: bfloat16 [1600, 256, 300], P('slab', 'panel'), may hold values from -18 to 18
- occ_energy: float32 [40], replicated, may hold values from -1 to -0.3
- vir_energy: float32 [300], replicated, may hold values from 0.1 to 2
- shift: float32 [1], replicated, may hold values from 0.5 to 1.5
Outputs:
- sigma: bfloat16 [1600, 256, 300], P('slab', 'panel')
- update: bfloat16 [1600, 256, 300], P('slab', 'panel')
- correlations: float32 [2], replicated
All inputs are finite; a program needn't handle non-finite values.
Results may differ from a plain program's by a relative error of at most 0.0079.
Values may be sent and summed in bfloat16 or wider, within the bound.
No kernel may reach another device: no remote copies, remote signals or barrier semaphores. Data moves between devices by JAX's collectives and lax.ppermute only.
A program may use at most 128 MiB of HBM per device.

v0:
```python
import jax
import jax.numpy as jnp
from jax import lax
from jax.sharding import PartitionSpec as P

OCCUPIED = 40


def per_device(trial, integrals, basis, images, current, occ_energy, vir_energy, shift):
    rows = trial.shape[0]
    width_b = integrals.shape[1]
    virtuals = integrals.shape[2]
    flat = integrals.reshape(integrals.shape[0], width_b * virtuals)
    whole = lax.all_gather(trial, "panel", axis=1, tiled=True)
    summed = jnp.dot(whole, flat, preferred_element_type=jnp.float32)
    sigma = summed.astype(jnp.bfloat16).reshape(rows, width_b, virtuals)
    sig_full = sigma.astype(jnp.float32)
    count = basis.shape[0]
    local_over = jnp.einsum(
        "kn,n->k", basis.reshape(count, -1), sigma.reshape(-1), preferred_element_type=jnp.float32
    )
    global_row = lax.axis_index("slab") * rows + jnp.arange(rows, dtype=jnp.int32)
    first_occ = global_row // OCCUPIED
    second_occ = global_row % OCCUPIED
    orbitals = jnp.arange(OCCUPIED, dtype=jnp.int32)
    energy_first = jnp.sum(
        jnp.where(first_occ[:, None] == orbitals[None, :], occ_energy[None, :], 0.0), axis=1
    )
    energy_second = jnp.sum(
        jnp.where(second_occ[:, None] == orbitals[None, :], occ_energy[None, :], 0.0), axis=1
    )
    pair_energy = energy_first + energy_second
    energy_b = lax.dynamic_slice_in_dim(vir_energy, lax.axis_index("panel") * width_b, width_b, 0)
    denom = jnp.maximum(
        vir_energy[None, None, :] + energy_b[None, :, None] - pair_energy[:, None, None] - shift[0],
        1.0,
    )
    scaled_current = current.astype(jnp.float32)
    correlations = lax.psum(local_over, ("slab", "panel"))
    resid = sig_full - shift[0] * scaled_current
    for index in range(count):
        resid = resid - correlations[index] * images[index].astype(jnp.float32)
    delta = resid / denom
    size_sq = lax.psum(jnp.sum(delta * delta), ("slab", "panel"))
    update = (delta * lax.rsqrt(size_sq + 1e-06)).astype(jnp.bfloat16)
    return (sigma, update, correlations)


def solution(mesh):
    in_specs = (
        P("slab", "panel"),
        P(None, "panel", None),
        P(None, "slab", "panel", None),
        P(None, "slab", "panel", None),
        P("slab", "panel", None),
        P(),
        P(),
        P(),
    )
    out_specs = (P("slab", "panel", None), P("slab", "panel", None), P())
    return jax.shard_map(
        per_device, mesh=mesh, in_specs=in_specs, out_specs=out_specs, check_vma=False
    )
```

profile of v0, /device:TPU:1, one launch (start us, length us, event | category | flops | bytes accessed | tf_op | source)
XLA Modules:
  0.0 309.0 jit_solution(7445834770455601225)
XLA Ops:
  7.2 0.0 all-gather.3.cloned.1.call-start
  7.2 0.7 all-gather.3.cloned.1.call-update
  7.9 15.1 %copy.16 = bf16[6400,4,300]{0,2,1:T(8,128)(2,1)} copy(bf16[6400,4,300]{0,1,2:T(4,128)(2,1)} %param.9) | data formatting | bytes 30720000 | tf_op args[1]
  23.0 16.0 %reshape.77 = bf16[6400,1200]{0,1:T(8,128)(2,1)} reshape(bf16[6400,4,300]{0,2,1:T(8,128)(2,1)} %copy.16) | data formatting | bytes 30720000 | tf_op jit(solution)/shard_map/reshape | solution.py:13
  39.0 5.8 %reshape.85 = bf16[960000]{0:T(1024)(128)(2,1)S(1)} reshape(bf16[2,400,4,300]{3,2,1,0:T(4,128)(2,1)} %param.10) | data formatting | bytes 3840000
  44.8 0.0 copy-start.3
  44.8 0.0 copy-start.1
  44.8 4.0 %reshape.79 = bf16[2,480000]{1,0:T(2,128)(2,1)} reshape(bf16[960000]{0:T(1024)(128)(2,1)S(1)} %reshape.85) | data formatting | bytes 3840000 | tf_op jit(solution)/shard_map/reshape | solution.py:20
  49.5 0.0 copy-done.3
  49.5 0.1 select_reduce_fusion
  49.6 0.0 copy-done.1
  49.6 0.1 dynamic_slice.3
  49.7 0.1 broadcast_add_fusion
  49.8 45.9 %all-gather.3.cloned.1.call-done = bf16[64,100,400]{1,2,0:T(8,128)(2,1)} async-done(((bf16[1,100,400]{1,2,0:T(8,128)(2,1)}), bf16[64,100,400]{1,2,0:T(8,128)(2,1)}) %all-gather.3.cloned.1.call-update) | async-done | bytes 5120016 | tf_op jit(solution)/shard_map/all_gather | solution.py:14
  95.7 7.3 %copy.15 = bf16[64,100,400]{1,0,2:T(8,128)(2,1)} copy(bf16[64,100,400]{1,2,0:T(8,128)(2,1)} %all-gather.3.cloned.1.call-done) | data formatting | bytes 10240000 | tf_op jit(solution)/shard_map/all_gather | solution.py:14
  103.0 13.1 %reshape.81 = bf16[6400,400]{0,1:T(8,128)(2,1)} reshape(bf16[64,100,400]{1,0,2:T(8,128)(2,1)} %copy.15) | data formatting | bytes 10240000
  116.1 15.8 %convolution_convert_fusion = bf16[400,1200]{1,0:T(8,128)(2,1)S(1)} fusion(bf16[6400,400]{0,1:T(8,128)(2,1)} %reshape.81, bf16[6400,1200]{0,1:T(8,128)(2,1)} %reshape.77), kind=kOutput, calls=%fused_computation | convolution fusion | flops 6144480256 | bytes 21440000 | tf_op jit(solution)/shard_map/dot_general | solution.py:15
  131.9 0.0 copy-start
  131.9 4.6 %reshape.82 = bf16[480000,1]{0,1:T(2,128)(2,1)} reshape(bf16[400,1200]{1,0:T(8,128)(2,1)S(1)} %convolution_convert_fusion) | data formatting | bytes 1920000 | tf_op jit(solution)/shard_map/reshape;reshape | solution.py:20
  136.6 0.0 copy-done
  136.6 5.6 %convolution_bitcast_fusion = f32[2]{0:T(128)S(1)} fusion(bf16[480000,1]{0,1:T(2,128)(2,1)} %reshape.82, bf16[2,480000]{1,0:T(2,128)(2,1)S(1)} %copy-done), kind=kOutput, calls=%fused_computation.6 | convolution fusion | flops 1920000 | bytes 2880008 | tf_op jit(solution)/shard_map/kn,n->k/dot_general | solution.py:19
  142.2 2.0 reshape.78
  144.2 74.6 %psum.14 = f32[2]{0:T(128)S(1)} all-reduce(f32[2]{0:T(128)S(1)} %convolution_bitcast_fusion), channel_id=1, replica_groups=mesh['slab'=4,'panel'=64] {'slab','panel'}, use_global_device_ids=true, to_apply=%region_0.1 | all-reduce | flops 2 | bytes 16 | tf_op jit(solution)/shard_map/psum | solution.py:39
  218.7 0.0 copy-start.2
  218.7 0.7 fusion.7
  219.4 7.3 %multiply_reduce_fusion = (f32[]{:T(128)}, f32[400,4,300]{2,1,0:T(4,128)S(1)}) fusion(f32[400]{0:T(512)S(1)} %add.70, f32[4,300]{1,0:T(4,128)S(1)} %broadcast_add_fusion, bf16[2,400,4,300]{3,2,1,0:T(4,128)(2,1)} %param.11, f32[]{:T(128)} %bitcast.6, f32[]{:T(128)} %bitcast.4, bf16[400,4,300]{2,1,0:T(4,128)(2,1)} %param.12, f32[]{:T(128)} %bitcast.26, ...), kind=kLoop, calls=%fused_computation.5 | loop fusion | flops 7679999 | bytes 5766416 | tf_op jit(solution)/shard_map/reduce_sum | solution.py:44
  226.7 0.0 copy-done.2
  226.7 73.4 %psum.15 = f32[]{:T(128)} all-reduce(f32[]{:T(128)} %get-tuple-element.5), channel_id=1, replica_groups=mesh['slab'=4,'panel'=64] {'slab','panel'}, use_global_device_ids=true, to_apply=%region_4.5 | all-reduce | flops 1 | bytes 8 | tf_op jit(solution)/shard_map/psum | solution.py:44
  300.7 1.5 multiply_convert_fusion
  (2 shorter events, 0.0 us)
Async XLA Ops:
  7.2 88.5 %all-gather.3.cloned.1.call-start = ((), (), s32[]{:S(2)}) async-start(), calls=%async_computation | async-start | bytes 6656000 | tf_op jit(solution)/shard_map/all_gather | solution.py:14
  44.8 4.7 %copy-start.3 = (f32[40]{0:T(128)S(1)}, f32[40]{0:T(128)}, u32[]{:S(2)}) copy-start(f32[40]{0:T(128)} %param.13) | copy-start | bytes 484
  44.8 4.8 %copy-start.1 = (f32[300]{0:T(512)S(1)}, f32[300]{0:T(512)}, u32[]{:S(2)}) copy-start(f32[300]{0:T(512)} %param.14) | copy-start | bytes 3604
  131.9 4.6 %copy-start = (bf16[2,480000]{1,0:T(2,128)(2,1)S(1)}, bf16[2,480000]{1,0:T(2,128)(2,1)}, u32[]{:S(2)}) copy-start(bf16[2,480000]{1,0:T(2,128)(2,1)} %reshape.79) | copy-start | bytes 5760004
  218.7 7.9 %copy-start.2 = (f32[2]{0:T(128)}, f32[2]{0:T(128)S(1)}, u32[]{:S(2)}) copy-start(f32[2]{0:T(128)S(1)} %psum.14) | copy-start | bytes 28
Sparse Core Ops, SparseCore 0:
  10.7 85.0 all-gather.2
where the time goes:
time: 310 us; the launch traced here: 309 us
  blocking collectives  148 us (48%)
  local copies, waits for them, and re-layouts  68.7 us (22%)
  waiting for transfers between devices  46.6 us (15%)
  matrix products  21.4 us (7%)
  between operations  15.5 us (5%)
  other arithmetic  8.91 us (3%)
    psum x1, blocking collectives, per_device(): correlations = lax.psum(local_over, ('slab', 'panel'))  74.6 us
    psum x1, blocking collectives, per_device(): size_sq = lax.psum(jnp.sum(delta * delta), ('slab', 'panel'))  73.4 us
    all_gather x1, waiting for transfers between devices, per_device(): whole = lax.all_gather(trial, 'panel', axis=1, tiled=True)  45.9 us
    unnamed x11, local copies, waits for them, and re-layouts  34 us
    reshape x1, local copies, waits for them, and re-layouts, per_device(): flat = integrals.reshape(integrals.shape[0], width_b * virtuals)  16 us
    dot_general x1, matrix products, per_device(): summed = jnp.dot(whole, flat, preferred_element_type=jnp.float32)  15.8 us
    all_gather x1, local copies, waits for them, and re-layouts, per_device(): whole = lax.all_gather(trial, 'panel', axis=1, tiled=True)  7.3 us
    reduce_sum x1, other arithmetic, per_device(): size_sq = lax.psum(jnp.sum(delta * delta), ('slab', 'panel'))  7.26 us
  transfers between devices with their start and end apart: 1, of which 1 were waited for; matrix products, arithmetic and copies ran while one was open for 13% of the time, Pallas kernels for 0%

commit v1 on v0

--- a/solution.py
+++ b/solution.py
@@ -11,7 +11,15 @@
     width_b = integrals.shape[1]
     virtuals = integrals.shape[2]
     flat = integrals.reshape(integrals.shape[0], width_b * virtuals)
-    whole = lax.all_gather(trial, "panel", axis=1, tiled=True)
+    whole = jnp.concatenate(
+        jax.lax.all_to_all(
+            jnp.stack([trial for _ in range(jax.lax.axis_size("panel"))]),
+            "panel",
+            split_axis=0,
+            concat_axis=0,
+        ),
+        axis=1,
+    )
     summed = jnp.dot(whole, flat, preferred_element_type=jnp.float32)
     sigma = summed.astype(jnp.bfloat16).reshape(rows, width_b, virtuals)
     sig_full = sigma.astype(jnp.float32)

time: 310 us -> 373 us (1.20)
  waiting for transfers between devices: 46.6 us -> 103 us
  between operations: 15.5 us -> 2.07 us
  starting transfers between devices: 0.04 us -> 13.3 us
  local copies, waits for them, and re-layouts: 68.7 us -> 73.1 us
    all_to_all x0 -> x1, waiting for transfers between devices: none -> 103 us  [per_device(): jax.lax.all_to_all(jnp.stack([trial for _ in range(jax.lax.axis_size('pan...]
    all_gather x1 -> x0, waiting for transfers between devices: 45.9 us -> none  [per_device(): whole = lax.all_gather(trial, 'panel', axis=1, tiled=True)]
    reshape x0 -> x2, local copies, waits for them, and re-layouts: none -> 20.4 us  [per_device(): jnp.concatenate(jax.lax.all_to_all(jnp.stack([trial for _ in range(jax.la...]
    all_to_all x0 -> x1, starting transfers between devices: none -> 13.3 us  [per_device(): jax.lax.all_to_all(jnp.stack([trial for _ in range(jax.lax.axis_size('pan...]
    unnamed x11 -> x10, local copies, waits for them, and re-layouts: 34 us -> 20.9 us
    all_gather x1 -> x0, local copies, waits for them, and re-layouts: 7.3 us -> none  [per_device(): whole = lax.all_gather(trial, 'panel', axis=1, tiled=True)]
    another operation x0 -> x1, local copies, waits for them, and re-layouts: none -> 4.47 us  [per_device(): jnp.stack([trial for _ in range(jax.lax.axis_size('panel'))])]
  transfers between devices with their start and end apart: 1 -> 1, of which waited for: 1 -> 1; matrix products, arithmetic and copies ran while one was open for 13% -> 11% of each run, Pallas kernels for 0% -> 0%
where the time goes in v1:
time: 373 us; the launch traced here: 372 us
  blocking collectives  150 us (40%)
  waiting for transfers between devices  103 us (28%)
  local copies, waits for them, and re-layouts  73.1 us (20%)
  matrix products  21.4 us (6%)
  starting transfers between devices  13.3 us (4%)
  other arithmetic  8.91 us (2%)
    all_to_all x1, waiting for transfers between devices, per_device(): jax.lax.all_to_all(jnp.stack([trial for _ in range(jax.lax.axis_size('pan...  103 us
    psum x1, blocking collectives, per_device(): correlations = lax.psum(local_over, ('slab', 'panel'))  77.7 us
    psum x1, blocking collectives, per_device(): size_sq = lax.psum(jnp.sum(delta * delta), ('slab', 'panel'))  72.7 us
    unnamed x10, local copies, waits for them, and re-layouts  20.9 us
    reshape x2, local copies, waits for them, and re-layouts, per_device(): jnp.concatenate(jax.lax.all_to_all(jnp.stack([trial for _ in range(jax.la...  20.4 us
    reshape x1, local copies, waits for them, and re-layouts, per_device(): flat = integrals.reshape(integrals.shape[0], width_b * virtuals)  16 us
    dot_general x1, matrix products, per_device(): summed = jnp.dot(whole, flat, preferred_element_type=jnp.float32)  15.8 us
    all_to_all x1, starting transfers between devices, per_device(): jax.lax.all_to_all(jnp.stack([trial for _ in range(jax.lax.axis_size('pan...  13.3 us
  transfers between devices with their start and end apart: 1, of which 1 were waited for; matrix products, arithmetic and copies ran while one was open for 11% of the time, Pallas kernels for 0%

profile of v1, /device:TPU:1, one launch (start us, length us, event | category | flops | bytes accessed | tf_op | source)
XLA Modules:
  0.0 371.7 jit_solution(4186195578989407305)
XLA Ops:
  0.6 4.5 %stack.2 = bf16[64,400,100]{2,1,0:T(8,128)(2,1)} broadcast(bf16[400,100]{1,0:T(8,128)(2,1)} %param.8), dimensions={1,2} | broadcast | bytes 5200000 | tf_op jit(solution)/shard_map/stack | solution.py:16
  5.1 13.3 %all-to-all-start = ((bf16[64,400,100]{2,1,0:T(8,128)(2,1)}), bf16[64,400,100]{2,1,0:T(8,128)(2,1)}, u32[]{:S(2)}, u32[]{:S(2)}) async-start(bf16[64,400,100]{2,1,0:T(8,128)(2,1)} %stack.2), calls=%async_computation | async-start | bytes 13107200 | tf_op jit(solution)/shard_map/all_to_all | solution.py:15
  18.4 15.1 %copy.15 = bf16[6400,4,300]{0,2,1:T(8,128)(2,1)} copy(bf16[6400,4,300]{0,1,2:T(4,128)(2,1)} %param.9) | data formatting | bytes 30720000 | tf_op args[1]
  33.5 16.0 %reshape.87 = bf16[6400,1200]{0,1:T(8,128)(2,1)} reshape(bf16[6400,4,300]{0,2,1:T(8,128)(2,1)} %copy.15) | data formatting | bytes 30720000 | tf_op jit(solution)/shard_map/reshape | solution.py:13
  49.5 5.8 %reshape.93 = bf16[960000]{0:T(1024)(128)(2,1)S(1)} reshape(bf16[2,400,4,300]{3,2,1,0:T(4,128)(2,1)} %param.10) | data formatting | bytes 3840000
  55.3 0.0 copy-start.3
  55.3 0.0 copy-start.1
  55.3 4.0 %reshape.89 = bf16[2,480000]{1,0:T(2,128)(2,1)} reshape(bf16[960000]{0:T(1024)(128)(2,1)S(1)} %reshape.93) | data formatting | bytes 3840000 | tf_op jit(solution)/shard_map/reshape | solution.py:28
  60.0 0.0 copy-done.3
  60.0 0.1 select_reduce_fusion
  60.1 0.0 copy-done.1
  60.1 0.1 dynamic_slice.3
  60.2 0.1 broadcast_add_fusion
  60.3 102.5 %all-to-all-done = bf16[64,400,100]{2,1,0:T(8,128)(2,1)} async-done(((bf16[64,400,100]{2,1,0:T(8,128)(2,1)}), bf16[64,400,100]{2,1,0:T(8,128)(2,1)}, u32[]{:S(2)}, u32[]{:S(2)}) %all-to-all-start) | async-done | bytes 5120032 | tf_op jit(solution)/shard_map/all_to_all | solution.py:15
  162.8 7.3 %copy.14 = bf16[400,64,100]{2,1,0:T(8,128)(2,1)} copy(bf16[400,64,100]{2,0,1:T(8,128)(2,1)} %bitcast) | data formatting | bytes 10240000 | tf_op jit(solution)/shard_map/reshape | solution.py:14
  170.1 13.1 %reshape.86 = bf16[400,6400]{1,0:T(8,128)(2,1)} reshape(bf16[400,64,100]{2,1,0:T(8,128)(2,1)} %copy.14) | data formatting | bytes 10240000 | tf_op jit(solution)/shard_map/reshape | solution.py:14
  183.2 15.8 %convolution_convert_fusion = bf16[400,1200]{1,0:T(8,128)(2,1)S(1)} fusion(bf16[400,6400]{1,0:T(8,128)(2,1)} %reshape.86, bf16[6400,1200]{0,1:T(8,128)(2,1)} %reshape.87), kind=kOutput, calls=%fused_computation | convolution fusion | flops 6144480256 | bytes 21440000 | tf_op jit(solution)/shard_map/dot_general | solution.py:23
  199.1 0.0 copy-start
  199.1 4.6 %reshape.90 = bf16[480000,1]{0,1:T(2,128)(2,1)} reshape(bf16[400,1200]{1,0:T(8,128)(2,1)S(1)} %convolution_convert_fusion) | data formatting | bytes 1920000 | tf_op jit(solution)/shard_map/reshape;reshape | solution.py:28
  203.7 0.0 copy-done
  203.7 5.6 %convolution_bitcast_fusion = f32[2]{0:T(128)S(1)} fusion(bf16[480000,1]{0,1:T(2,128)(2,1)} %reshape.90, bf16[2,480000]{1,0:T(2,128)(2,1)S(1)} %copy-done), kind=kOutput, calls=%fused_computation.6 | convolution fusion | flops 1920000 | bytes 2880008 | tf_op jit(solution)/shard_map/kn,n->k/dot_general | solution.py:27
  209.3 2.0 reshape.88
  211.3 77.7 %psum.14 = f32[2]{0:T(128)S(1)} all-reduce(f32[2]{0:T(128)S(1)} %convolution_bitcast_fusion), channel_id=1, replica_groups=mesh['slab'=4,'panel'=64] {'slab','panel'}, use_global_device_ids=true, to_apply=%region_0.1 | all-reduce | flops 2 | bytes 16 | tf_op jit(solution)/shard_map/psum | solution.py:47
  289.0 0.0 copy-start.2
  289.0 0.7 fusion.7
  289.6 7.3 %multiply_reduce_fusion = (f32[]{:T(128)}, f32[400,4,300]{2,1,0:T(4,128)S(1)}) fusion(f32[400]{0:T(512)S(1)} %add.70, f32[4,300]{1,0:T(4,128)S(1)} %broadcast_add_fusion, bf16[2,400,4,300]{3,2,1,0:T(4,128)(2,1)} %param.11, f32[]{:T(128)} %bitcast.5, f32[]{:T(128)} %bitcast.3, bf16[400,4,300]{2,1,0:T(4,128)(2,1)} %param.12, f32[]{:T(128)} %bitcast.22, ...), kind=kLoop, calls=%fused_computation.5 | loop fusion | flops 7679999 | bytes 5766416 | tf_op jit(solution)/shard_map/reduce_sum | solution.py:52
  296.9 0.0 copy-done.2
  296.9 72.7 %psum.15 = f32[]{:T(128)} all-reduce(f32[]{:T(128)} %get-tuple-element.5), channel_id=1, replica_groups=mesh['slab'=4,'panel'=64] {'slab','panel'}, use_global_device_ids=true, to_apply=%region_4.5 | all-reduce | flops 1 | bytes 8 | tf_op jit(solution)/shard_map/psum | solution.py:52
  370.3 1.5 multiply_convert_fusion
  (2 shorter events, 0.0 us)
Async XLA Ops:
  5.1 157.7 %all-to-all-start = ((bf16[64,400,100]{2,1,0:T(8,128)(2,1)}), bf16[64,400,100]{2,1,0:T(8,128)(2,1)}, u32[]{:S(2)}, u32[]{:S(2)}) async-start(bf16[64,400,100]{2,1,0:T(8,128)(2,1)} %stack.2), calls=%async_computation | async-start | bytes 13107200 | tf_op jit(solution)/shard_map/all_to_all | solution.py:15
  55.3 4.7 %copy-start.3 = (f32[40]{0:T(128)S(1)}, f32[40]{0:T(128)}, u32[]{:S(2)}) copy-start(f32[40]{0:T(128)} %param.13) | copy-start | bytes 484
  55.3 4.8 %copy-start.1 = (f32[300]{0:T(512)S(1)}, f32[300]{0:T(512)}, u32[]{:S(2)}) copy-start(f32[300]{0:T(512)} %param.14) | copy-start | bytes 3604
  199.1 4.6 %copy-start = (bf16[2,480000]{1,0:T(2,128)(2,1)S(1)}, bf16[2,480000]{1,0:T(2,128)(2,1)}, u32[]{:S(2)}) copy-start(bf16[2,480000]{1,0:T(2,128)(2,1)} %reshape.89) | copy-start | bytes 5760004
  289.0 7.9 %copy-start.2 = (f32[2]{0:T(128)}, f32[2]{0:T(128)S(1)}, u32[]{:S(2)}) copy-start(f32[2]{0:T(128)S(1)} %psum.14) | copy-start | bytes 28
